TPU v7x, 256 devices: a whole 4x4x8 slice. The times are simulated.
256 devices in a mesh: sx: 8 (over z_hi, x), sy: 4 (over z_lo), af: 8 (over y, core).
Axes of the slice: x: 4, y: 4, z: 8 (z_hi: 2, z_lo: 4; z = z_hi * 4 + z_lo), core: 2. Of those that a mesh axis runs over, the one named last changes fastest.
Arguments:
- volume: bfloat16 [8, 48, 48, 48, 128], P('af', 'sx', 'sy'), may hold values from -6 to 6
- kernel: bfloat16 [3, 3, 3, 128, 256], P(None, None, None, 'sx', ('sy', 'af')), may hold values from -0.109375 to 0.109375
- cotangent: bfloat16 [8, 256, 24, 576], P('sx', ('sy', 'af')), may hold values from -6 to 6
Outputs:
- features: bfloat16 [8, 256, 24, 576], P('sx', ('sy', 'af'))
- volume_grad: bfloat16 [8, 48, 48, 48, 128], P('af', 'sx', 'sy')
- kernel_grad: float32 [3, 3, 3, 128, 256], P(None, None, None, 'sx', ('sy', 'af'))
All inputs are finite; a program needn't handle non-finite values.
Results may differ from a plain program's by a relative error of at most 0.0025.
Values may be sent and summed in bfloat16 or wider, within the bound.
A program may use at most 64 MiB of HBM per device.

v0:
```python
import jax
import jax.numpy as jnp
from jax import lax
from jax.sharding import PartitionSpec as P


def from_behind(value, axis, steps):
    count = lax.axis_size(axis)
    leading, last = (max(0, -steps), min(count, count - steps))
    return lax.ppermute(value, axis, [(source, source + steps) for source in range(leading, last)])


def strided_patch(extended, tap_d, tap_h, tap_w, depth, height, width):
    return extended[
        :,
        tap_d : tap_d + 2 * depth : 2,
        tap_h : tap_h + 2 * height : 2,
        tap_w : tap_w + 2 * width : 2,
        :,
    ]


def parity_view(extended):
    samples, d_ext, h_ext, w_ext, channels = extended.shape
    pads = [(0, 0)] + [(0, n % 2) for n in (d_ext, h_ext, w_ext)] + [(0, 0)]
    even = jnp.pad(extended, pads)
    _, d2, h2, w2, _ = even.shape
    split = even.reshape(samples, d2 // 2, 2, h2 // 2, 2, w2 // 2, 2, channels)
    return split.transpose(2, 4, 6, 0, 1, 3, 5, 7)


def im2col(classes, depth, height, width):
    patches = []
    for tap_d in range(3):
        for tap_h in range(3):
            for tap_w in range(3):
                cls = classes[tap_d % 2, tap_h % 2, tap_w % 2]
                od, oh, ow = (tap_d // 2, tap_h // 2, tap_w // 2)
                patches.append(cls[:, od : od + depth, oh : oh + height, ow : ow + width, :])
    return jnp.concatenate(patches, axis=-1)


def weave(even_part, odd_part, axis):
    stacked = jnp.stack([even_part, odd_part], axis=axis + 1)
    shape = list(even_part.shape)
    shape[axis] = shape[axis] * 2
    return stacked.reshape(shape)


def spread_back(grad_space, kernel_full):
    samples, depth, height, width, filters = grad_space.shape
    channels = kernel_full.shape[3]
    grad_flat = grad_space.reshape(-1, filters)
    classes = {}
    for tap_d in range(3):
        for tap_h in range(3):
            for tap_w in range(3):
                term = lax.dot_general(
                    grad_flat,
                    kernel_full[tap_d, tap_h, tap_w],
                    (((1,), (1,)), ((), ())),
                    preferred_element_type=jnp.float32,
                )
                term = term.reshape(samples, depth, height, width, channels)
                pads = [(0, 0)]
                for tap in (tap_d, tap_h, tap_w):
                    pads.append((1, 0) if tap == 2 else (0, 1))
                pads.append((0, 0))
                term = jnp.pad(term, pads)
                key_name = (tap_d % 2, tap_h % 2, tap_w % 2)
                classes[key_name] = classes[key_name] + term if key_name in classes else term
    planes = []
    for parity_d in range(2):
        rows_h = []
        for parity_h in range(2):
            rows_h.append(weave(classes[parity_d, parity_h, 0], classes[parity_d, parity_h, 1], 3))
        planes.append(weave(rows_h[0], rows_h[1], 2))
    whole = weave(planes[0], planes[1], 1)
    return whole[:, : 2 * depth + 1, : 2 * height + 1, : 2 * width + 1, :]


def on_device(volume, kernel, cotangent):
    samples = volume.shape[0]
    depth = volume.shape[1] // 2
    height = volume.shape[2] // 2
    width = volume.shape[3] // 2
    n_sy = lax.axis_size("sy")
    n_af = lax.axis_size("af")
    kernel_part = lax.all_gather(kernel, ("sy", "af"), axis=4, tiled=True)
    kernel_full = lax.all_gather(kernel_part, "sx", axis=3, tiled=True)
    filters = kernel_full.shape[4]
    per_dev = filters // (n_sy * n_af)
    below = from_behind(volume[:, -1:], "sx", 1)
    extended = jnp.concatenate([below, volume], axis=1)
    beside = from_behind(extended[:, :, -1:], "sy", 1)
    extended = jnp.concatenate([beside, extended], axis=2)
    extended = jnp.pad(extended, ((0, 0), (0, 0), (0, 0), (1, 0), (0, 0)))
    rows = samples * depth * height * width
    classes = parity_view(extended)
    cols = im2col(classes, depth, height, width).reshape(rows, -1)
    kernel_mat = kernel_full.reshape(-1, filters)
    total = jnp.dot(cols, kernel_mat, preferred_element_type=jnp.float32)
    conv_space = total.astype(jnp.bfloat16).reshape(
        samples, depth, height, width, n_sy, n_af, per_dev
    )
    by_sample = lax.all_to_all(conv_space, "af", split_axis=5, concat_axis=0, tiled=True)
    gathered = lax.all_to_all(
        lax.all_to_all(by_sample, "sx", split_axis=0, concat_axis=1, tiled=True),
        "sy",
        split_axis=4,
        concat_axis=2,
        tiled=True,
    )
    own_samples = gathered.shape[0]
    edge_d = gathered.shape[1]
    edge_h = gathered.shape[2]
    features = (
        gathered.reshape(own_samples, edge_d, edge_h, width, per_dev)
        .transpose(0, 4, 1, 2, 3)
        .reshape(own_samples, per_dev, edge_d, edge_h * width)
    )
    grad_after = (
        cotangent.reshape(own_samples, per_dev, edge_d, edge_h, width)
        .transpose(0, 2, 3, 4, 1)
        .reshape(own_samples, edge_d, edge_h, width, 1, 1, per_dev)
    )
    grad_region = lax.all_to_all(
        lax.all_to_all(grad_after, "sx", split_axis=1, concat_axis=0, tiled=True),
        "sy",
        split_axis=2,
        concat_axis=4,
        tiled=True,
    )
    grad_back = lax.all_to_all(grad_region, "af", split_axis=0, concat_axis=5, tiled=True)
    grad_space = grad_back.reshape(samples, depth, height, width, filters)
    grad_flat = grad_space.reshape(rows, filters)
    kernel_terms = lax.dot_general(
        cols, grad_flat, (((0,), (0,)), ((), ())), preferred_element_type=jnp.float32
    )
    n_sx = lax.axis_size("sx")
    channels = kernel_full.shape[3]
    taps = kernel_terms.reshape(27, channels, n_sy * n_af, per_dev).transpose(2, 0, 1, 3)
    by_filter = lax.all_to_all(taps, ("sy", "af"), 0, 0, tiled=True).sum(axis=0)
    own_ch = channels // n_sx
    by_filter = by_filter.reshape(27, n_sx, own_ch, per_dev).transpose(1, 0, 2, 3)
    kernel_grad = lax.all_to_all(by_filter, "sx", 0, 0, tiled=True).sum(axis=0)
    kernel_grad = kernel_grad.reshape(3, 3, 3, own_ch, per_dev)
    partial_grad = spread_back(grad_space, kernel_full)
    from_above = from_behind(partial_grad[:, 0:1], "sx", -1)
    own_depth = partial_grad[:, 1:]
    own_depth = jnp.concatenate([own_depth[:, :-1], own_depth[:, -1:] + from_above], axis=1)
    from_right = from_behind(own_depth[:, :, 0:1].astype(jnp.bfloat16), "sy", -1).astype(
        jnp.float32
    )
    own_height = own_depth[:, :, 1:]
    own_height = jnp.concatenate(
        [own_height[:, :, :-1], own_height[:, :, -1:] + from_right], axis=2
    )
    volume_grad = own_height[:, :, :, 1:]
    return (features, volume_grad.astype(jnp.bfloat16), kernel_grad)


def solution(mesh):
    return jax.shard_map(
        on_device,
        mesh=mesh,
        in_specs=(
            P("af", "sx", "sy", None, None),
            P(None, None, None, "sx", ("sy", "af")),
            P("sx", ("sy", "af"), None, None),
        ),
        out_specs=(
            P("sx", ("sy", "af"), None, None),
            P("af", "sx", "sy", None, None),
            P(None, None, None, "sx", ("sy", "af")),
        ),
        check_vma=False,
    )
```

profile of v0, /device:TPU:96, one launch (start us, length us, event | category | flops | bytes accessed | tf_op | source)
XLA Modules:
  0.0 357.8 jit_solution(4887128388619679048)
XLA Ops:
  9.3 3.4 collective-permute-start
  12.8 6.2 %collective-permute-done = bf16[1,1,12,48,128]{4,1,3,2,0:T(2,128)(2,1)S(1)} collective-permute-done((bf16[1,1,12,48,128]{4,1,3,2,0:T(2,128)(2,1)S(1)}, bf16[1,1,12,48,128]{4,1,3,2,0:T(2,128)(2,1)S(1)}, u32[]{:S(2)}, u32[]{:S(2)}) %collective-permute-start) | collective-permute-done | bytes 147488 | tf_op jit(solution)/shard_map/ppermute | solution.py:10
  21.0 40.2 %all_gather.6 = bf16[3,3,3,16,256]{3,4,2,1,0:T(8,128)(2,1)S(1)} all-gather(bf16[3,3,3,16,8]{3,4,2,1,0:T(8,128)(2,1)S(1)} %copy-done.8), channel_id=1, replica_groups=mesh['sx'=8,'sy'=4,'af'=8] {'sy','af'}, dimensions={4}, use_global_device_ids=true | all-gather | bytes 228096 | tf_op jit(solution)/shard_map/all_gather | solution.py:89
  67.7 18.5 %all-to-all-start.3 = ((bf16[8,2,6912]{2,1,0:T(2,128)(2,1)}), bf16[8,2,6912]{2,1,0:T(2,128)(2,1)S(1)}, u32[]{:S(2)}, u32[]{:S(2)}) async-start(bf16[8,2,6912]{2,1,0:T(2,128)(2,1)} %reshape.261), calls=%async_computation.3 | async-start | bytes 442368 | tf_op jit(solution)/shard_map/all_to_all | solution.py:128
  112.7 12.0 %all-to-all-start.4 = ((bf16[4,2,13824]{2,1,0:T(2,128)(2,1)}), bf16[4,2,13824]{2,1,0:T(2,128)(2,1)S(1)}, u32[]{:S(2)}, u32[]{:S(2)}) async-start(bf16[4,2,13824]{2,1,0:T(2,128)(2,1)} %reshape.263), calls=%async_computation.4 | async-start | bytes 442368 | tf_op jit(solution)/shard_map/all_to_all | solution.py:127
  126.2 10.7 %all-to-all-done.4 = bf16[4,2,13824]{2,1,0:T(2,128)(2,1)S(1)} async-done(((bf16[4,2,13824]{2,1,0:T(2,128)(2,1)}), bf16[4,2,13824]{2,1,0:T(2,128)(2,1)S(1)}, u32[]{:S(2)}, u32[]{:S(2)}) %all-to-all-start.4) | async-done | bytes 221216 | tf_op jit(solution)/shard_map/all_to_all | solution.py:127
  141.2 8.3 %all-to-all-start.5 = ((bf16[8,2,6912]{2,1,0:T(2,128)(2,1)}), bf16[8,2,6912]{2,1,0:T(2,128)(2,1)}, u32[]{:S(2)}, u32[]{:S(2)}) async-start(bf16[8,2,6912]{2,1,0:T(2,128)(2,1)} %reshape.265), calls=%async_computation.5 | async-start | bytes 442368 | tf_op jit(solution)/shard_map/all_to_all | solution.py:134
  150.2 4.0 %copy.581 = bf16[1,3,6,24,3456]{4,3,2,1,0:T(8,128)(2,1)} copy(bf16[1,3,6,24,3456]{4,1,3,2,0:T(4,128)(2,1)} %slice_dynamic-update-slice_fusion) | data formatting | bytes 5971968 | tf_op jit(solution)/shard_map/concatenate | solution.py:40
  154.2 4.3 %dot_general.205 = bf16[27,128,432]{1,0,2:T(8,128)(2,1)S(1)} reshape(bf16[3456,432]{0,1:T(8,128)(2,1)} %bitcast.438) | data formatting | bytes 5971968 | tf_op jit(solution)/shard_map/dot_general | solution.py:137
  158.5 3.6 %reshape.266 = bf16[8,1,3,4,6,8,24]{6,5,4,3,2,1,0:T(8,128)(2,1)} reshape(bf16[8,2,6912]{2,1,0:T(2,128)(2,1)} %all-to-all-done.5) | data formatting | bytes 442368
  162.2 4.0 %convolution_convert_fusion = bf16[432,256]{1,0:T(8,128)(2,1)} fusion(bf16[432,3456]{1,0:T(8,128)(2,1)} %bitcast.439, bf16[3456,256]{1,0:T(8,128)(2,1)} %bitcast.458), kind=kOutput, calls=%fused_computation.16 | convolution fusion | flops 764522496 | bytes 4976640 | tf_op jit(solution)/shard_map/dot_general | solution.py:102
  168.0 2.8 reshape.217
  170.8 2.7 copy.724
  173.5 3.5 reshape.255
  177.0 4.8 %all-to-all-start = ((bf16[8,2,6912]{2,1,0:T(2,128)(2,1)}), bf16[8,2,6912]{2,1,0:T(2,128)(2,1)}, u32[]{:S(2)}, u32[]{:S(2)}) async-start(bf16[8,2,6912]{2,1,0:T(2,128)(2,1)} %reshape.255), calls=%async_computation | async-start | bytes 442368 | tf_op jit(solution)/shard_map/all_to_all | solution.py:106
  185.8 2.8 reshape_reshape.4
  189.0 3.6 %reshape.256 = bf16[8,1,3,6,4,8,24]{6,5,4,3,2,1,0:T(8,128)(2,1)} reshape(bf16[8,2,6912]{2,1,0:T(2,128)(2,1)} %all-to-all-done) | data formatting | bytes 442368
  195.2 3.5 reshape.257
  198.7 9.4 %all-to-all-start.1 = ((bf16[8,2,6912]{2,1,0:T(2,128)(2,1)}), bf16[8,2,6912]{2,1,0:T(2,128)(2,1)}, u32[]{:S(2)}, u32[]{:S(2)}) async-start(bf16[8,2,6912]{2,1,0:T(2,128)(2,1)} %reshape.257), calls=%async_computation.1 | async-start | bytes 442368 | tf_op jit(solution)/shard_map/all_to_all | solution.py:108
  210.4 3.9 %copy.631 = f32[32,27,128,8]{2,3,1,0:T(8,128)} copy(f32[32,27,128,8]{2,0,3,1:T(8,128)S(1)} %fusion.6) | data formatting | bytes 7077888 | tf_op jit(solution)/shard_map/transpose | solution.py:142
  214.2 4.9 %all-to-all-done.1 = bf16[8,2,6912]{2,1,0:T(2,128)(2,1)} async-done(((bf16[8,2,6912]{2,1,0:T(2,128)(2,1)}), bf16[8,2,6912]{2,1,0:T(2,128)(2,1)}, u32[]{:S(2)}, u32[]{:S(2)}) %all-to-all-start.1) | async-done | bytes 221216 | tf_op jit(solution)/shard_map/all_to_all | solution.py:108
  219.1 8.7 %all-to-all-start.6 = ((f32[32,27,128,8]{2,3,1,0:T(8,128)}), f32[32,27,128,8]{2,3,1,0:T(8,128)}, u32[]{:S(2)}, u32[]{:S(2)}) async-start(f32[32,27,128,8]{2,3,1,0:T(8,128)} %copy.631), calls=%async_computation.6 | async-start | bytes 7077888 | tf_op jit(solution)/shard_map/all_to_all | solution.py:143
  249.8 3.6 %reshape.258 = bf16[8,3,6,4,1,8,24]{6,5,4,3,2,1,0:T(8,128)(2,1)} reshape(bf16[8,2,6912]{2,1,0:T(2,128)(2,1)} %all-to-all-done.1) | data formatting | bytes 442368
  253.5 2.5 copy_bitcast_fusion.10
  256.0 3.5 reshape.259
  259.5 53.2 %all-to-all-done.6 = f32[32,27,128,8]{2,3,1,0:T(8,128)} async-done(((f32[32,27,128,8]{2,3,1,0:T(8,128)}), f32[32,27,128,8]{2,3,1,0:T(8,128)}, u32[]{:S(2)}, u32[]{:S(2)}) %all-to-all-start.6) | async-done | bytes 3538976 | tf_op jit(solution)/shard_map/all_to_all | solution.py:143
  312.7 5.9 %all-to-all-start.2 = ((bf16[4,2,13824]{2,1,0:T(2,128)(2,1)}), bf16[4,2,13824]{2,1,0:T(2,128)(2,1)}, u32[]{:S(2)}, u32[]{:S(2)}) async-start(bf16[4,2,13824]{2,1,0:T(2,128)(2,1)} %reshape.259), calls=%async_computation.2 | async-start | bytes 442368 | tf_op jit(solution)/shard_map/all_to_all | solution.py:107
  322.2 3.1 collective-permute-start.3
  326.5 2.8 reduce_sum.18
  334.1 3.6 %all-to-all-start.7 = ((f32[8,1,3456]{2,1,0:T(1,128)}), f32[8,1,3456]{2,1,0:T(1,128)S(1)}, u32[]{:S(2)}, u32[]{:S(2)}) async-start(f32[8,1,3456]{2,1,0:T(1,128)} %reshape.267), calls=%async_computation.7 | async-start | bytes 221184 | tf_op jit(solution)/shard_map/all_to_all | solution.py:146
  340.3 2.9 reshape.260
  345.0 3.0 all-to-all-done.7
  (148 shorter events, 92.8 us)
Async XLA Ops:
  7.2 13.9 %copy-start.8 = (bf16[3,3,3,16,8]{3,4,2,1,0:T(8,128)(2,1)S(1)}, bf16[3,3,3,16,8]{3,4,2,1,0:T(8,128)(2,1)}, u32[]{:S(2)}) copy-start(bf16[3,3,3,16,8]{3,4,2,1,0:T(8,128)(2,1)} %param.4) | copy-start | bytes 20740
  7.2 155.0 %all-gather.2.cloned.1.call-start = ((), (), s32[]{:S(2)}) async-start(), calls=%async_computation.8 | async-start | bytes 1990656 | tf_op jit(solution)/shard_map/all_gather | solution.py:90
  9.3 9.7 %collective-permute-start = (bf16[1,1,12,48,128]{4,1,3,2,0:T(2,128)(2,1)S(1)}, bf16[1,1,12,48,128]{4,1,3,2,0:T(2,128)(2,1)S(1)}, u32[]{:S(2)}, u32[]{:S(2)}) collective-permute-start(bf16[1,1,12,48,128]{4,1,3,2,0:T(2,128)(2,1)S(1)} %slice.315), channel_id=1, source_target_pairs={{0,32},{32,64},{64,96},{96,128},{128,160},{160,192},{192,224},{1,3... | collective-permute-start | bytes 442376 | tf_op jit(solution)/shard_map/ppermute | solution.py:10
  19.0 0.7 copy-start.6
  19.7 66.5 %collective-permute-start.1 = (bf16[1,7,1,48,128]{4,1,3,2,0:T(8,128)(2,1)}, bf16[1,7,1,48,128]{4,1,3,2,0:T(8,128)(2,1)}, u32[]{:S(2)}, u32[]{:S(2)}) collective-permute-start(bf16[1,7,1,48,128]{4,1,3,2,0:T(8,128)(2,1)} %pad_maximum_fusion.9), channel_id=1, source_target_pairs={{0,8},{8,16},{16,24},{1,9},{9,17},{17,25},{2,10},{10,18},{18,26},{... | collective-permute-start | bytes 258056 | tf_op jit(solution)/shard_map/ppermute | solution.py:10
  65.5 20.7 %copy-start.7 = (bf16[1,1,12,48,128]{4,1,3,2,0:T(2,128)(2,1)S(1)}, bf16[1,1,12,48,128]{4,1,3,2,0:T(2,128)(2,1)}, u32[]{:S(2)}) copy-start(bf16[1,1,12,48,128]{4,1,3,2,0:T(2,128)(2,1)} %copy-done.6) | copy-start | bytes 442372
  67.7 40.8 %all-to-all-start.3 = ((bf16[8,2,6912]{2,1,0:T(2,128)(2,1)}), bf16[8,2,6912]{2,1,0:T(2,128)(2,1)S(1)}, u32[]{:S(2)}, u32[]{:S(2)}) async-start(bf16[8,2,6912]{2,1,0:T(2,128)(2,1)} %reshape.261), calls=%async_computation.3 | async-start | bytes 442368 | tf_op jit(solution)/shard_map/all_to_all | solution.py:128
  112.7 24.2 %all-to-all-start.4 = ((bf16[4,2,13824]{2,1,0:T(2,128)(2,1)}), bf16[4,2,13824]{2,1,0:T(2,128)(2,1)S(1)}, u32[]{:S(2)}, u32[]{:S(2)}) async-start(bf16[4,2,13824]{2,1,0:T(2,128)(2,1)} %reshape.263), calls=%async_computation.4 | async-start | bytes 442368 | tf_op jit(solution)/shard_map/all_to_all | solution.py:127
  141.2 17.4 %all-to-all-start.5 = ((bf16[8,2,6912]{2,1,0:T(2,128)(2,1)}), bf16[8,2,6912]{2,1,0:T(2,128)(2,1)}, u32[]{:S(2)}, u32[]{:S(2)}) async-start(bf16[8,2,6912]{2,1,0:T(2,128)(2,1)} %reshape.265), calls=%async_computation.5 | async-start | bytes 442368 | tf_op jit(solution)/shard_map/all_to_all | solution.py:134
  177.0 12.0 %all-to-all-start = ((bf16[8,2,6912]{2,1,0:T(2,128)(2,1)}), bf16[8,2,6912]{2,1,0:T(2,128)(2,1)}, u32[]{:S(2)}, u32[]{:S(2)}) async-start(bf16[8,2,6912]{2,1,0:T(2,128)(2,1)} %reshape.255), calls=%async_computation | async-start | bytes 442368 | tf_op jit(solution)/shard_map/all_to_all | solution.py:106
  183.2 1.0 copy-start.1
  198.7 20.4 %all-to-all-start.1 = ((bf16[8,2,6912]{2,1,0:T(2,128)(2,1)}), bf16[8,2,6912]{2,1,0:T(2,128)(2,1)}, u32[]{:S(2)}, u32[]{:S(2)}) async-start(bf16[8,2,6912]{2,1,0:T(2,128)(2,1)} %reshape.257), calls=%async_computation.1 | async-start | bytes 442368 | tf_op jit(solution)/shard_map/all_to_all | solution.py:108
  214.2 13.6 %copy-start.2 = (bf16[1,3,6,24,4,8,1,8]{3,7,2,4,1,5,6,0:T(8,128)(2,1)S(1)}, bf16[1,3,6,24,4,8,1,8]{3,7,2,4,1,5,6,0:T(8,128)(2,1)}, u32[]{:S(2)}) copy-start(bf16[1,3,6,24,4,8,1,8]{3,7,2,4,1,5,6,0:T(8,128)(2,1)} %copy-done.1) | copy-start | bytes 663556
  219.1 93.5 %all-to-all-start.6 = ((f32[32,27,128,8]{2,3,1,0:T(8,128)}), f32[32,27,128,8]{2,3,1,0:T(8,128)}, u32[]{:S(2)}, u32[]{:S(2)}) async-start(f32[32,27,128,8]{2,3,1,0:T(8,128)} %copy.631), calls=%async_computation.6 | async-start | bytes 7077888 | tf_op jit(solution)/shard_map/all_to_all | solution.py:143
  227.8 1.5 copy-start.5
  247.9 1.6 copy-start
  248.1 70.4 %collective-permute-start.2 = (f32[1,1,13,49,128]{4,1,3,2,0:T(1,128)S(1)}, f32[1,1,13,49,128]{4,1,3,2,0:T(1,128)S(1)}, u32[]{:S(2)}, u32[]{:S(2)}) collective-permute-start(f32[1,1,13,49,128]{4,1,3,2,0:T(1,128)S(1)} %slice.380), channel_id=1, source_target_pairs={{32,0},{64,32},{96,64},{128,96},{160,128},{192,160},{224,192},{33,... | collective-permute-start | bytes 978440 | tf_op jit(solution)/shard_map/ppermute | solution.py:10
  312.7 21.4 %all-to-all-start.2 = ((bf16[4,2,13824]{2,1,0:T(2,128)(2,1)}), bf16[4,2,13824]{2,1,0:T(2,128)(2,1)}, u32[]{:S(2)}, u32[]{:S(2)}) async-start(bf16[4,2,13824]{2,1,0:T(2,128)(2,1)} %reshape.259), calls=%async_computation.2 | async-start | bytes 442368 | tf_op jit(solution)/shard_map/all_to_all | solution.py:107
  320.8 0.7 copy-start.4
  322.2 15.6 %collective-permute-start.3 = (bf16[1,6,1,49,128]{4,1,3,2,0:T(8,128)(2,1)}, bf16[1,6,1,49,128]{4,1,3,2,0:T(8,128)(2,1)}, u32[]{:S(2)}, u32[]{:S(2)}) collective-permute-start(bf16[1,6,1,49,128]{4,1,3,2,0:T(8,128)(2,1)} %slice.384), channel_id=1, source_target_pairs={{8,0},{16,8},{24,16},{9,1},{17,9},{25,17},{10,2},{18,10},{26,18},{... | collective-permute-start | bytes 225800 | tf_op jit(solution)/shard_map/ppermute | solution.py:10
  334.1 13.9 %all-to-all-start.7 = ((f32[8,1,3456]{2,1,0:T(1,128)}), f32[8,1,3456]{2,1,0:T(1,128)S(1)}, u32[]{:S(2)}, u32[]{:S(2)}) async-start(f32[8,1,3456]{2,1,0:T(1,128)} %reshape.267), calls=%async_computation.7 | async-start | bytes 221184 | tf_op jit(solution)/shard_map/all_to_all | solution.py:146
  337.7 1.3 copy-start.3
Sparse Core Ops, SparseCore 0:
  62.8 88.7 all-gather.1
where the time goes:
time: 364 us; the launch traced here: 358 us
  local copies, waits for them, and re-layouts  113 us (31%)
  starting transfers between devices  80.2 us (22%)
  waiting for transfers between devices  78.5 us (22%)
  blocking collectives  40.2 us (11%)
  matrix products  18.7 us (5%)
  between operations  14.8 us (4%)
  other arithmetic  12.6 us (3%)
    unnamed x66, local copies, waits for them, and re-layouts  67.3 us
    all_to_all x1, waiting for transfers between devices, on_device(): by_filter = lax.all_to_all(taps, ('sy', 'af'), 0, 0, tiled=True).sum(axis=0)  53.2 us
    all_gather x1, blocking collectives, on_device(): kernel_part = lax.all_gather(kernel, ('sy', 'af'), axis=4, tiled=True)  40.2 us
    all_to_all x1, starting transfers between devices, on_device(): lax.all_to_all(grad_after, 'sx', split_axis=1, concat_axis=0, tiled=True)  18.5 us
    dot_general x27, matrix products, spread_back(): lax.dot_general(grad_flat, kernel_full[tap_d, tap_h, tap_w], (((1,), (1,)...  12.4 us
    all_to_all x1, starting transfers between devices, on_device(): lax.all_to_all(lax.all_to_all(grad_after, 'sx', split_axis=1, concat_axis...  12 us
    all_to_all x1, waiting for transfers between devices, on_device(): lax.all_to_all(lax.all_to_all(grad_after, 'sx', split_axis=1, concat_axis...  10.7 us
    all_to_all x1, starting transfers between devices, on_device(): lax.all_to_all(by_sample, 'sx', split_axis=0, concat_axis=1, tiled=True)  9.37 us
  transfers between devices with their start and end apart: 13, of which 6 were waited for; matrix products, arithmetic and copies ran while one was open for 31% of the time, Pallas kernels for 0%

commit v1 on v0

--- a/solution.py
+++ b/solution.py
@@ -104,12 +104,20 @@
         samples, depth, height, width, n_sy, n_af, per_dev
     )
     by_sample = lax.all_to_all(conv_space, "af", split_axis=5, concat_axis=0, tiled=True)
-    gathered = lax.all_to_all(
-        lax.all_to_all(by_sample, "sx", split_axis=0, concat_axis=1, tiled=True),
-        "sy",
-        split_axis=4,
-        concat_axis=2,
-        tiled=True,
+    gathered = jnp.concatenate(
+        lax.all_to_all(
+            jnp.stack(
+                jnp.split(
+                    lax.all_to_all(by_sample, "sx", split_axis=0, concat_axis=1, tiled=True),
+                    lax.axis_size("sy"),
+                    axis=4,
+                )
+            ),
+            "sy",
+            0,
+            0,
+        ),
+        axis=2,
     )
     own_samples = gathered.shape[0]
     edge_d = gathered.shape[1]

time: 364 us -> 352 us (0.967)
  the two profiles are of different devices: /device:TPU:96 before, /device:TPU:32 now
where the time goes in v1:
time: 352 us; the launch traced here: 346 us
  waiting for transfers between devices  99.7 us (28%)
  local copies, waits for them, and re-layouts  81.6 us (23%)
  starting transfers between devices  78.7 us (22%)
  blocking collectives  39.2 us (11%)
  matrix products  21.2 us (6%)
  between operations  14.8 us (4%)
  other arithmetic  10.5 us (3%)
    ppermute x4, waiting for transfers between devices, from_behind(): lax.ppermute(value, axis, [(source, source + steps) for source in range(l...  69.9 us
    unnamed x59, local copies, waits for them, and re-layouts  50.1 us
    all_gather x1, blocking collectives, on_device(): kernel_part = lax.all_gather(kernel, ('sy', 'af'), axis=4, tiled=True)  39.2 us
    all_to_all x1, starting transfers between devices, on_device(): lax.all_to_all(grad_after, 'sx', split_axis=1, concat_axis=0, tiled=True)  20.6 us
    dot_general x27, matrix products, spread_back(): lax.dot_general(grad_flat, kernel_full[tap_d, tap_h, tap_w], (((1,), (1,)...  15.4 us
    all_to_all x1, waiting for transfers between devices, on_device(): lax.all_to_all(lax.all_to_all(grad_after, 'sx', split_axis=1, concat_axis...  11 us
    ppermute x4, starting transfers between devices, from_behind(): lax.ppermute(value, axis, [(source, source + steps) for source in range(l...  10.7 us
    all_to_all x1, starting transfers between devices, on_device(): lax.all_to_all(lax.all_to_all(grad_after, 'sx', split_axis=1, concat_axis...  9.57 us
  transfers between devices with their start and end apart: 13, of which 9 were waited for; matrix products, arithmetic and copies ran while one was open for 25% of the time, Pallas kernels for 0%

profile of v1, /device:TPU:32, one launch (start us, length us, event | category | flops | bytes accessed | tf_op | source)
XLA Modules:
  0.0 345.7 jit_solution(1032100684447806204)
XLA Ops:
  9.3 3.4 collective-permute-start
  12.8 6.2 %collective-permute-done = bf16[1,1,12,48,128]{4,1,3,2,0:T(2,128)(2,1)S(1)} collective-permute-done((bf16[1,1,12,48,128]{4,1,3,2,0:T(2,128)(2,1)S(1)}, bf16[1,1,12,48,128]{4,1,3,2,0:T(2,128)(2,1)S(1)}, u32[]{:S(2)}, u32[]{:S(2)}) %collective-permute-start) | collective-permute-done | bytes 147488 | tf_op jit(solution)/shard_map/ppermute | solution.py:10
  19.7 3.8 %collective-permute-start.1 = (bf16[1,7,1,48,128]{4,1,3,2,0:T(8,128)(2,1)}, bf16[1,7,1,48,128]{4,1,3,2,0:T(8,128)(2,1)}, u32[]{:S(2)}, u32[]{:S(2)}) collective-permute-start(bf16[1,7,1,48,128]{4,1,3,2,0:T(8,128)(2,1)} %pad_maximum_fusion.10), channel_id=1, source_target_pairs={{0,8},{8,16},{16,24},{1,9},{9,17},{17,25},{2,10},{10,18},{18,26},{... | collective-permute-start | bytes 258056 | tf_op jit(solution)/shard_map/ppermute | solution.py:10
  23.6 39.2 %all_gather.6 = bf16[3,3,3,16,256]{3,4,2,1,0:T(8,128)(2,1)S(1)} all-gather(bf16[3,3,3,16,8]{3,4,2,1,0:T(8,128)(2,1)S(1)} %copy-done.5), channel_id=1, replica_groups=mesh['sx'=8,'sy'=4,'af'=8] {'sy','af'}, dimensions={4}, use_global_device_ids=true | all-gather | bytes 228096 | tf_op jit(solution)/shard_map/all_gather | solution.py:89
  67.0 2.2 reshape.260
  69.2 20.6 %all-to-all-start.3 = ((bf16[8,2,6912]{2,1,0:T(2,128)(2,1)}), bf16[8,2,6912]{2,1,0:T(2,128)(2,1)S(1)}, u32[]{:S(2)}, u32[]{:S(2)}) async-start(bf16[8,2,6912]{2,1,0:T(2,128)(2,1)} %reshape.260), calls=%async_computation.3 | async-start | bytes 442368 | tf_op jit(solution)/shard_map/all_to_all | solution.py:136
  114.1 2.2 reshape.262
  116.4 9.6 %all-to-all-start.4 = ((bf16[4,2,13824]{2,1,0:T(2,128)(2,1)}), bf16[4,2,13824]{2,1,0:T(2,128)(2,1)S(1)}, u32[]{:S(2)}, u32[]{:S(2)}) async-start(bf16[4,2,13824]{2,1,0:T(2,128)(2,1)} %reshape.262), calls=%async_computation.4 | async-start | bytes 442368 | tf_op jit(solution)/shard_map/all_to_all | solution.py:135
  127.5 11.0 %all-to-all-done.4 = bf16[4,2,13824]{2,1,0:T(2,128)(2,1)S(1)} async-done(((bf16[4,2,13824]{2,1,0:T(2,128)(2,1)}), bf16[4,2,13824]{2,1,0:T(2,128)(2,1)S(1)}, u32[]{:S(2)}, u32[]{:S(2)}) %all-to-all-start.4) | async-done | bytes 221216 | tf_op jit(solution)/shard_map/all_to_all | solution.py:135
  140.5 2.2 reshape.264
  142.7 8.4 %all-to-all-start.5 = ((bf16[8,2,6912]{2,1,0:T(2,128)(2,1)}), bf16[8,2,6912]{2,1,0:T(2,128)(2,1)S(1)}, u32[]{:S(2)}, u32[]{:S(2)}) async-start(bf16[8,2,6912]{2,1,0:T(2,128)(2,1)} %reshape.264), calls=%async_computation.5 | async-start | bytes 442368 | tf_op jit(solution)/shard_map/all_to_all | solution.py:142
  151.9 2.4 copy.614
  154.3 3.6 %dot_general.205 = bf16[27,128,432]{1,0,2:T(8,128)(2,1)} reshape(bf16[3456,432]{0,1:T(8,128)(2,1)S(1)} %bitcast.447) | data formatting | bytes 5971968 | tf_op jit(solution)/shard_map/dot_general | solution.py:145
  158.2 2.7 reshape.265
  160.9 2.4 convolution_convert_fusion
  165.8 3.5 %reshape.254 = bf16[8,2,6912]{2,1,0:T(2,128)(2,1)} reshape(bf16[8,1,3,6,4,8,24]{6,5,4,3,2,1,0:T(8,128)(2,1)} %bitcast.459) | data formatting | bytes 442368
  169.4 4.5 %all-to-all-start = ((bf16[8,2,6912]{2,1,0:T(2,128)(2,1)}), bf16[8,2,6912]{2,1,0:T(2,128)(2,1)S(1)}, u32[]{:S(2)}, u32[]{:S(2)}) async-start(bf16[8,2,6912]{2,1,0:T(2,128)(2,1)} %reshape.254), calls=%async_computation | async-start | bytes 442368 | tf_op jit(solution)/shard_map/all_to_all | solution.py:106
  176.3 4.7 %all-to-all-done = bf16[8,2,6912]{2,1,0:T(2,128)(2,1)S(1)} async-done(((bf16[8,2,6912]{2,1,0:T(2,128)(2,1)}), bf16[8,2,6912]{2,1,0:T(2,128)(2,1)S(1)}, u32[]{:S(2)}, u32[]{:S(2)}) %all-to-all-start) | async-done | bytes 221216 | tf_op jit(solution)/shard_map/all_to_all | solution.py:106
  182.9 2.2 reshape.256
  185.1 8.0 %all-to-all-start.1 = ((bf16[8,2,6912]{2,1,0:T(2,128)(2,1)}), bf16[8,2,6912]{2,1,0:T(2,128)(2,1)S(1)}, u32[]{:S(2)}, u32[]{:S(2)}) async-start(bf16[8,2,6912]{2,1,0:T(2,128)(2,1)} %reshape.256), calls=%async_computation.1 | async-start | bytes 442368 | tf_op jit(solution)/shard_map/all_to_all | solution.py:111
  193.1 3.4 fusion.6
  196.5 3.8 %copy.666 = f32[32,27,128,8]{2,3,1,0:T(8,128)} copy(f32[32,27,128,8]{2,0,3,1:T(8,128)S(1)} %fusion.6) | data formatting | bytes 7077888 | tf_op jit(solution)/shard_map/transpose | solution.py:150
  201.6 2.5 all-to-all-done.1
  206.2 2.2 reshape.258
  208.5 6.1 %all-to-all-start.2 = ((bf16[4,2,13824]{2,1,0:T(2,128)(2,1)}), bf16[4,2,13824]{2,1,0:T(2,128)(2,1)S(1)}, u32[]{:S(2)}, u32[]{:S(2)}) async-start(bf16[4,2,13824]{2,1,0:T(2,128)(2,1)} %reshape.258), calls=%async_computation.2 | async-start | bytes 442368 | tf_op jit(solution)/shard_map/all_to_all | solution.py:108
  217.7 2.8 all-to-all-done.2
  220.5 5.4 %all-to-all-start.6 = ((f32[32,27,128,8]{2,3,1,0:T(8,128)}), f32[32,27,128,8]{2,3,1,0:T(8,128)}, u32[]{:S(2)}, u32[]{:S(2)}) async-start(f32[32,27,128,8]{2,3,1,0:T(8,128)} %copy.666), calls=%async_computation.6 | async-start | bytes 7077888 | tf_op jit(solution)/shard_map/all_to_all | solution.py:151
  245.9 10.1 %collective-permute-done.2 = f32[1,1,13,49,128]{4,1,3,2,0:T(1,128)S(1)} collective-permute-done((f32[1,1,13,49,128]{4,1,3,2,0:T(1,128)S(1)}, f32[1,1,13,49,128]{4,1,3,2,0:T(1,128)S(1)}, u32[]{:S(2)}, u32[]{:S(2)}) %collective-permute-start.2) | collective-permute-done | bytes 326176 | tf_op jit(solution)/shard_map/ppermute | solution.py:10
  257.1 2.2 collective-permute-start.3
  259.6 53.6 %collective-permute-done.3 = bf16[1,6,1,49,128]{4,1,3,2,0:T(8,128)(2,1)S(1)} collective-permute-done((bf16[1,6,1,49,128]{4,1,3,2,0:T(8,128)(2,1)S(1)}, bf16[1,6,1,49,128]{4,1,3,2,0:T(8,128)(2,1)S(1)}, u32[]{:S(2)}, u32[]{:S(2)}) %collective-permute-start.3) | collective-permute-done | bytes 75296 | tf_op jit(solution)/shard_map/ppermute | solution.py:10
  320.5 5.2 %all-to-all-start.7 = ((f32[8,1,3456]{2,1,0:T(1,128)}), f32[8,1,3456]{2,1,0:T(1,128)S(1)}, u32[]{:S(2)}, u32[]{:S(2)}) async-start(f32[8,1,3456]{2,1,0:T(1,128)} %reshape.266), calls=%async_computation.7 | async-start | bytes 221184 | tf_op jit(solution)/shard_map/all_to_all | solution.py:154
  327.5 8.5 %all-to-all-done.7 = f32[8,1,3456]{2,1,0:T(1,128)S(1)} async-done(((f32[8,1,3456]{2,1,0:T(1,128)}), f32[8,1,3456]{2,1,0:T(1,128)S(1)}, u32[]{:S(2)}, u32[]{:S(2)}) %all-to-all-start.7) | async-done | bytes 110624 | tf_op jit(solution)/shard_map/all_to_all | solution.py:154
  (144 shorter events, 81.9 us)
Async XLA Ops:
  7.2 16.4 %copy-start.5 = (bf16[3,3,3,16,8]{3,4,2,1,0:T(8,128)(2,1)S(1)}, bf16[3,3,3,16,8]{3,4,2,1,0:T(8,128)(2,1)}, u32[]{:S(2)}) copy-start(bf16[3,3,3,16,8]{3,4,2,1,0:T(8,128)(2,1)} %param.4) | copy-start | bytes 20740
  7.2 153.7 %all-gather.2.cloned.1.call-start = ((), (), s32[]{:S(2)}) async-start(), calls=%async_computation.8 | async-start | bytes 1990656 | tf_op jit(solution)/shard_map/all_gather | solution.py:90
  9.3 9.7 %collective-permute-start = (bf16[1,1,12,48,128]{4,1,3,2,0:T(2,128)(2,1)S(1)}, bf16[1,1,12,48,128]{4,1,3,2,0:T(2,128)(2,1)S(1)}, u32[]{:S(2)}, u32[]{:S(2)}) collective-permute-start(bf16[1,1,12,48,128]{4,1,3,2,0:T(2,128)(2,1)S(1)} %slice.315), channel_id=1, source_target_pairs={{0,32},{32,64},{64,96},{96,128},{128,160},{160,192},{192,224},{1,3... | collective-permute-start | bytes 442376 | tf_op jit(solution)/shard_map/ppermute | solution.py:10
  19.0 0.7 copy-start.2
  19.7 70.1 %collective-permute-start.1 = (bf16[1,7,1,48,128]{4,1,3,2,0:T(8,128)(2,1)}, bf16[1,7,1,48,128]{4,1,3,2,0:T(8,128)(2,1)}, u32[]{:S(2)}, u32[]{:S(2)}) collective-permute-start(bf16[1,7,1,48,128]{4,1,3,2,0:T(8,128)(2,1)} %pad_maximum_fusion.10), channel_id=1, source_target_pairs={{0,8},{8,16},{16,24},{1,9},{9,17},{17,25},{2,10},{10,18},{18,26},{... | collective-permute-start | bytes 258056 | tf_op jit(solution)/shard_map/ppermute | solution.py:10
  67.0 22.9 %copy-start.3 = (bf16[1,1,12,48,128]{4,1,3,2,0:T(2,128)(2,1)S(1)}, bf16[1,1,12,48,128]{4,1,3,2,0:T(2,128)(2,1)}, u32[]{:S(2)}) copy-start(bf16[1,1,12,48,128]{4,1,3,2,0:T(2,128)(2,1)} %copy-done.2) | copy-start | bytes 442372
  69.2 42.9 %all-to-all-start.3 = ((bf16[8,2,6912]{2,1,0:T(2,128)(2,1)}), bf16[8,2,6912]{2,1,0:T(2,128)(2,1)S(1)}, u32[]{:S(2)}, u32[]{:S(2)}) async-start(bf16[8,2,6912]{2,1,0:T(2,128)(2,1)} %reshape.260), calls=%async_computation.3 | async-start | bytes 442368 | tf_op jit(solution)/shard_map/all_to_all | solution.py:136
  116.4 22.1 %all-to-all-start.4 = ((bf16[4,2,13824]{2,1,0:T(2,128)(2,1)}), bf16[4,2,13824]{2,1,0:T(2,128)(2,1)S(1)}, u32[]{:S(2)}, u32[]{:S(2)}) async-start(bf16[4,2,13824]{2,1,0:T(2,128)(2,1)} %reshape.262), calls=%async_computation.4 | async-start | bytes 442368 | tf_op jit(solution)/shard_map/all_to_all | solution.py:135
  142.7 15.5 %all-to-all-start.5 = ((bf16[8,2,6912]{2,1,0:T(2,128)(2,1)}), bf16[8,2,6912]{2,1,0:T(2,128)(2,1)S(1)}, u32[]{:S(2)}, u32[]{:S(2)}) async-start(bf16[8,2,6912]{2,1,0:T(2,128)(2,1)} %reshape.264), calls=%async_computation.5 | async-start | bytes 442368 | tf_op jit(solution)/shard_map/all_to_all | solution.py:142
  164.5 9.4 %copy-start = (bf16[8,1,3,4,6,8,24]{6,5,4,3,2,1,0:T(8,128)(2,1)S(1)}, bf16[8,1,3,4,6,8,24]{6,5,4,3,2,1,0:T(8,128)(2,1)}, u32[]{:S(2)}) copy-start(bf16[8,1,3,4,6,8,24]{6,5,4,3,2,1,0:T(8,128)(2,1)} %reshape.265) | copy-start | bytes 663556
  169.4 11.6 %all-to-all-start = ((bf16[8,2,6912]{2,1,0:T(2,128)(2,1)}), bf16[8,2,6912]{2,1,0:T(2,128)(2,1)S(1)}, u32[]{:S(2)}, u32[]{:S(2)}) async-start(bf16[8,2,6912]{2,1,0:T(2,128)(2,1)} %reshape.254), calls=%async_computation | async-start | bytes 442368 | tf_op jit(solution)/shard_map/all_to_all | solution.py:106
  182.9 10.2 %copy-start.4 = (bf16[432,256]{0,1:T(8,128)(2,1)S(1)}, bf16[432,256]{0,1:T(8,128)(2,1)}, u32[]{:S(2)}) copy-start(bf16[432,256]{0,1:T(8,128)(2,1)} %reshape_reshape.8) | copy-start | bytes 663556
  185.1 18.9 %all-to-all-start.1 = ((bf16[8,2,6912]{2,1,0:T(2,128)(2,1)}), bf16[8,2,6912]{2,1,0:T(2,128)(2,1)S(1)}, u32[]{:S(2)}, u32[]{:S(2)}) async-start(bf16[8,2,6912]{2,1,0:T(2,128)(2,1)} %reshape.256), calls=%async_computation.1 | async-start | bytes 442368 | tf_op jit(solution)/shard_map/all_to_all | solution.py:111
  208.5 8.1 %copy-start.1 = (bf16[3,3,3,128,256]{4,3,2,1,0:T(8,128)(2,1)S(1)}, bf16[3,3,3,128,256]{4,3,2,1,0:T(8,128)(2,1)}, u32[]{:S(2)}) copy-start(bf16[3,3,3,128,256]{4,3,2,1,0:T(8,128)(2,1)} %all-gather.2.cloned.1.call-done) | copy-start | bytes 5308420
  208.5 12.0 %all-to-all-start.2 = ((bf16[4,2,13824]{2,1,0:T(2,128)(2,1)}), bf16[4,2,13824]{2,1,0:T(2,128)(2,1)S(1)}, u32[]{:S(2)}, u32[]{:S(2)}) async-start(bf16[4,2,13824]{2,1,0:T(2,128)(2,1)} %reshape.258), calls=%async_computation.2 | async-start | bytes 442368 | tf_op jit(solution)/shard_map/all_to_all | solution.py:108
  220.5 95.7 %all-to-all-start.6 = ((f32[32,27,128,8]{2,3,1,0:T(8,128)}), f32[32,27,128,8]{2,3,1,0:T(8,128)}, u32[]{:S(2)}, u32[]{:S(2)}) async-start(f32[32,27,128,8]{2,3,1,0:T(8,128)} %copy.666), calls=%async_computation.6 | async-start | bytes 7077888 | tf_op jit(solution)/shard_map/all_to_all | solution.py:151
  244.4 11.6 %collective-permute-start.2 = (f32[1,1,13,49,128]{4,1,3,2,0:T(1,128)S(1)}, f32[1,1,13,49,128]{4,1,3,2,0:T(1,128)S(1)}, u32[]{:S(2)}, u32[]{:S(2)}) collective-permute-start(f32[1,1,13,49,128]{4,1,3,2,0:T(1,128)S(1)} %slice.380), channel_id=1, source_target_pairs={{32,0},{64,32},{96,64},{128,96},{160,128},{192,160},{224,192},{33,... | collective-permute-start | bytes 978440 | tf_op jit(solution)/shard_map/ppermute | solution.py:10
  257.1 56.0 %collective-permute-start.3 = (bf16[1,6,1,49,128]{4,1,3,2,0:T(8,128)(2,1)S(1)}, bf16[1,6,1,49,128]{4,1,3,2,0:T(8,128)(2,1)S(1)}, u32[]{:S(2)}, u32[]{:S(2)}) collective-permute-start(bf16[1,6,1,49,128]{4,1,3,2,0:T(8,128)(2,1)S(1)} %slice.384), channel_id=1, source_target_pairs={{8,0},{16,8},{24,16},{9,1},{17,9},{25,17},{10,2},{18,10},{26,18},{... | collective-permute-start | bytes 225800 | tf_op jit(solution)/shard_map/ppermute | solution.py:10
  320.5 15.6 %all-to-all-start.7 = ((f32[8,1,3456]{2,1,0:T(1,128)}), f32[8,1,3456]{2,1,0:T(1,128)S(1)}, u32[]{:S(2)}, u32[]{:S(2)}) async-start(f32[8,1,3456]{2,1,0:T(1,128)} %reshape.266), calls=%async_computation.7 | async-start | bytes 221184 | tf_op jit(solution)/shard_map/all_to_all | solution.py:154
Sparse Core Ops, SparseCore 0:
  64.3 89.6 all-gather.1
